TPU v7x, 256 devices: a whole 4x4x8 slice. The times are simulated.
256 devices in a mesh: seq: 2 (over core), ctx: 64 (over x_lo, y, z), head: 2 (over x_hi).
Axes of the slice: x: 4 (x_hi: 2, x_lo: 2; x = x_hi * 2 + x_lo), y: 4, z: 8, core: 2. Of those that a mesh axis runs over, the one named last changes fastest.
Arguments:
- queries: bfloat16 [16384, 8, 128], P(('seq', 'ctx'), 'head'), parts along dimension 0, may hold values from -8 to 8
- key_rows: bfloat16 [16384, 128], P(('seq', 'ctx')), parts along dimension 0, may hold values from -8 to 8
- value_rows: bfloat16 [16384, 128], P(('seq', 'ctx')), parts along dimension 0, may hold values from -6 to 6
- out_grad: bfloat16 [16384, 8, 128], P(('seq', 'ctx'), 'head'), parts along dimension 0, may hold values from -6 to 6
- doc_lengths: int32 [16], P('seq'), parts along dimension 0, may hold values from 1 to 2048, 8192 in all
- balance: int32 [16384], P('seq'), parts along dimension 0, may hold values from 0 to 8191, as said below
Outputs:
- attended: bfloat16 [16384, 8, 128], P(('seq', 'ctx'), 'head'), parts along dimension 0
- query_grad: bfloat16 [16384, 8, 128], P(('seq', 'ctx'), 'head'), parts along dimension 0
- key_grad: bfloat16 [16384, 128], P(('seq', 'ctx')), parts along dimension 0
- value_grad: bfloat16 [16384, 128], P(('seq', 'ctx')), parts along dimension 0
There are 2 independent parts, one for each index of `seq`. A program takes and returns all parts, laid end to end along the dimension named above; each array names one. Nothing has to cross between parts.
Inputs may be any that keep to these rules, and one draw needn't show every extreme that they name: `doc_lengths`: the lengths sum to 8192 and the longest is exactly 2048. `balance`: A permutation of the positions that moves aligned runs of 64 positions whole and in order.
All inputs are finite; a program needn't handle non-finite values.
Results may differ from a plain program's by a relative error of at most 0.034.
Values may be sent and summed in bfloat16 or wider, within the bound.
A program may use at most 64 MiB of HBM per device.

v0:
```python
import math
import jax
import jax.numpy as jnp
from jax import lax
from jax.sharding import PartitionSpec as P

NEGATIVE = -1e30


def document_of(positions, doc_lengths):
    doc_ends = jnp.cumsum(doc_lengths)
    return jnp.sum((positions[:, None] >= doc_ends[None, :]).astype(jnp.int32), axis=1)


def body(queries, key_rows, value_rows, out_grad, doc_lengths, balance):
    tok_rows = queries.shape[0]
    heads_here = queries.shape[1]
    head_width = queries.shape[2]
    scaling = 1.0 / math.sqrt(head_width)
    seq_total = balance.shape[0]
    block_len = min(512, seq_total)
    block_count = seq_total // block_len
    docs_all = document_of(balance, doc_lengths)
    my_first = lax.axis_index("ctx") * tok_rows
    my_pos = lax.dynamic_slice_in_dim(balance, my_first, tok_rows)
    my_doc = lax.dynamic_slice_in_dim(docs_all, my_first, tok_rows)
    all_keys, all_values = (
        lax.all_gather(key_rows, "ctx", axis=0, tiled=True),
        lax.all_gather(value_rows, "ctx", axis=0, tiled=True),
    )

    def key_block(row_start):
        key_pos = lax.dynamic_slice_in_dim(balance, row_start, block_len)
        key_doc = lax.dynamic_slice_in_dim(docs_all, row_start, block_len)
        visible_pairs = (key_doc[None, :] == my_doc[:, None]) & (
            key_pos[None, :] <= my_pos[:, None]
        )
        key_blk = lax.dynamic_slice_in_dim(all_keys, row_start, block_len)
        value_blk = lax.dynamic_slice_in_dim(all_values, row_start, block_len)
        return (key_blk, value_blk, visible_pairs)

    def forward_step(step_index, state_now):
        key_blk, value_blk, visible_pairs = key_block(step_index * block_len)
        allowed = visible_pairs[:, None, :]
        running_max, weight_sum, weighted = state_now
        scores = (
            jnp.einsum("qhd,kd->qhk", queries, key_blk, preferred_element_type=jnp.float32)
            * scaling
        )
        scores = jnp.where(allowed, scores, NEGATIVE)
        new_max = jnp.maximum(running_max, jnp.max(scores, axis=2))
        raw_weights = jnp.where(allowed, jnp.exp(scores - new_max[:, :, None]), 0.0)
        factor = jnp.exp(running_max - new_max)
        weight_sum = weight_sum * factor + jnp.sum(raw_weights, axis=2)
        weighted = weighted * factor[:, :, None] + jnp.einsum(
            "qhk,kd->qhd",
            raw_weights.astype(jnp.bfloat16),
            value_blk,
            preferred_element_type=jnp.float32,
        )
        return (new_max, weight_sum, weighted)

    start_state = (
        jnp.full((tok_rows, heads_here), NEGATIVE, jnp.float32),
        jnp.zeros((tok_rows, heads_here), jnp.float32),
        jnp.zeros((tok_rows, heads_here, head_width), jnp.float32),
    )
    running_max, weight_sum, weighted = lax.fori_loop(0, block_count, forward_step, start_state)
    attended = (weighted / weight_sum[:, :, None]).astype(jnp.bfloat16)
    log_total = running_max + jnp.log(weight_sum)
    row_inner = jnp.sum(out_grad.astype(jnp.float32) * attended.astype(jnp.float32), axis=2)

    def backward_tile(query_part, grad_part, total_part, inner_part, key_blk, value_blk, allowed):
        scores = (
            jnp.einsum("qhd,kd->qhk", query_part, key_blk, preferred_element_type=jnp.float32)
            * scaling
        )
        weights = jnp.where(allowed, jnp.exp(scores - total_part[:, :, None]), 0.0)
        grad_weights = jnp.einsum(
            "qhd,kd->qhk", grad_part, value_blk, preferred_element_type=jnp.float32
        )
        grad_scores = (weights * (grad_weights - inner_part[:, :, None])).astype(jnp.bfloat16)
        return (weights.astype(jnp.bfloat16), grad_scores)

    def query_step(step_index, state_now):
        row_start = step_index * block_len
        key_blk, value_blk, visible_pairs = key_block(row_start)
        allowed = visible_pairs[:, None, :]
        grad_acc, key_terms = state_now
        weights_b, grad_scores = backward_tile(
            queries, out_grad, log_total, row_inner, key_blk, value_blk, allowed
        )
        grad_acc = grad_acc + jnp.einsum(
            "qhk,kd->qhd", grad_scores, key_blk, preferred_element_type=jnp.float32
        )
        key_part = (
            jnp.einsum("qhk,qhd->kd", grad_scores, queries, preferred_element_type=jnp.float32)
            * scaling
        )
        value_part = jnp.einsum(
            "qhk,qhd->kd", weights_b, out_grad, preferred_element_type=jnp.float32
        )
        key_terms = lax.dynamic_update_slice_in_dim(
            key_terms, jnp.concatenate([key_part, value_part], axis=1), row_start, 0
        )
        return (grad_acc, key_terms)

    grad_start = (
        jnp.zeros((tok_rows, heads_here, head_width), jnp.float32),
        jnp.zeros((seq_total, 2 * head_width), jnp.float32),
    )
    grad_acc, key_terms = lax.fori_loop(0, block_count, query_step, grad_start)
    query_grad = (grad_acc * scaling).astype(jnp.bfloat16)
    shared = lax.psum_scatter(key_terms, "ctx", scatter_dimension=0, tiled=True)
    combined = lax.psum(shared, "head")
    key_grad = combined[:, :head_width].astype(jnp.bfloat16)
    value_grad = combined[:, head_width:].astype(jnp.bfloat16)
    return (attended, query_grad, key_grad, value_grad)


def solution(mesh):
    return jax.shard_map(
        body,
        mesh=mesh,
        in_specs=(
            P(("seq", "ctx"), "head", None),
            P(("seq", "ctx"), None),
            P(("seq", "ctx"), None),
            P(("seq", "ctx"), "head", None),
            P("seq"),
            P("seq"),
        ),
        out_specs=(
            P(("seq", "ctx"), "head", None),
            P(("seq", "ctx"), "head", None),
            P(("seq", "ctx"), None),
            P(("seq", "ctx"), None),
        ),
        check_vma=False,
    )
```

profile of v0, /device:TPU:2, one launch (start us, length us, event | category | flops | bytes accessed | tf_op | source)
XLA Modules:
  0.0 1131.8 jit_solution(8781327198950465208)
XLA Ops:
  14.3 297.5 %all-gather.3.cloned.1.call-done = bf16[8192,128]{1,0:T(8,128)(2,1)} async-done(((bf16[128,128]{1,0:T(8,128)(2,1)}), bf16[8192,128]{1,0:T(8,128)(2,1)}) %all-gather.3.cloned.1.call-update) | async-done | bytes 2097168 | tf_op jit(solution)/shard_map/all_gather | solution.py:28
  311.8 299.0 %all-gather.5.cloned.1.call-done = bf16[8192,128]{1,0:T(8,128)(2,1)} async-done(((bf16[128,128]{1,0:T(8,128)(2,1)}), bf16[8192,128]{1,0:T(8,128)(2,1)}) %all-gather.5.cloned.1.call-update) | async-done | bytes 2097168 | tf_op jit(solution)/shard_map/all_gather | solution.py:29
  610.9 62.5 %while.34 = (s32[]{:T(128)}, f32[128,4]{0,1:T(4,128)S(1)}, f32[128,4]{0,1:T(4,128)S(1)}, f32[128,4,128]{2,0,1:T(8,128)S(1)}, s32[8192]{0:T(1024)S(1)}, /*index=5...) while((s32[]{:T(128)}, f32[128,4]{0,1:T(4,128)S(1)}, ...), condition=%wide.region_5.6_spmd.clone, body=%wide.region_2.5_spmd.clone.sunk | while | flops 136972800 | bytes 4371679 | solution.py:68
  613.4 1.3 convolution_add_fusion.4
  617.3 1.3 convolution_add_fusion.4
  621.2 1.3 convolution_add_fusion.4
  625.1 1.4 convolution_add_fusion.4
  629.0 1.3 convolution_add_fusion.4
  632.9 1.4 convolution_add_fusion.4
  636.8 1.3 convolution_add_fusion.4
  640.7 1.4 convolution_add_fusion.4
  644.6 1.3 convolution_add_fusion.4
  648.5 1.4 convolution_add_fusion.4
  652.4 1.3 convolution_add_fusion.4
  656.3 1.4 convolution_add_fusion.4
  660.2 1.3 convolution_add_fusion.4
  664.1 1.4 convolution_add_fusion.4
  668.0 1.3 convolution_add_fusion.4
  671.9 1.4 convolution_add_fusion.4
  674.4 3.8 broadcast_in_dim.114.clone
  678.2 104.2 %while.35 = (s32[]{:T(128)}, f32[128,4,128]{2,0,1:T(8,128)S(1)}, f32[8192,256]{1,0:T(8,128)}, s32[8192]{0:T(1024)S(1)}, s32[128]{0:T(128)S(1)}, /*index=5*/s32[8...) while((s32[]{:T(128)}, f32[128,4,128]{2,0,1:T(8,128)S(1)}, ...), condition=%wide.region_8.9_spmd.clone, body=%wide.region_7.8_spmd.clone.sunk | while | flops 337903616 | bytes 9979125 | solution.py:112
  695.0 1.3 convolution_add_fusion.5
  783.3 328.7 %reduce-scatter.2.cloned.1.call-done = f32[128,256]{1,0:T(8,128)} async-done(((f32[8192,256]{1,0:T(8,128)}), f32[128,256]{1,0:T(8,128)}) %reduce-scatter.2.cloned.1.call-update) | async-done | bytes 131088 | tf_op jit(solution)/shard_map/reduce_scatter | solution.py:114
  1112.0 12.7 %all-reduce.1 = bf16[128,256]{1,0:T(8,128)(2,1)S(1)} all-reduce(f32[128,256]{1,0:T(8,128)} %reduce-scatter.2.cloned.1.call-done), channel_id=1, replica_groups=mesh['seq'=2,'ctx'=64,'head'=2] {'head'}, use_global_device_ids=true, to_apply=%region_10.11 | all-reduce | flops 32768 | bytes 196608 | tf_op jit(solution)/shard_map/psum | solution.py:115
  (328 shorter events, 151.5 us)
Async XLA Ops:
  7.2 304.7 %all-gather.3.cloned.1.call-start = ((), (), s32[]{:S(2)}) async-start(), calls=%async_computation.1 | async-start | bytes 2129920 | tf_op jit(solution)/shard_map/all_gather | solution.py:28
  7.9 603.0 %all-gather.5.cloned.1.call-start = ((), (), s32[]{:S(2)}) async-start(), calls=%async_computation.2 | async-start | bytes 2129920 | tf_op jit(solution)/shard_map/all_gather | solution.py:29
  8.6 1103.4 %reduce-scatter.2.cloned.1.call-start = ((), (), s32[]{:S(2)}) async-start(), calls=%async_computation.3 | async-start | bytes 8519680 | tf_op jit(solution)/shard_map/reduce_scatter | solution.py:114
  610.9 62.6 %copy-start = (bf16[128,4,128]{2,1,0:T(4,128)(2,1)S(1)}, bf16[128,4,128]{2,1,0:T(4,128)(2,1)}, u32[]{:S(2)}) copy-start(bf16[128,4,128]{2,1,0:T(4,128)(2,1)} %param.13) | copy-start | bytes 393220
Sparse Core Ops, SparseCore 0:
  9.8 301.9 all-gather.2
  313.6 297.2 all-gather.4
  782.6 329.3 reduce-scatter.1
where the time goes:
time: 1130 us
  waiting for transfers between devices  927 us (82%)
  matrix products  110 us (10%)
  local copies, waits for them, and re-layouts  51.9 us (5%)
  other arithmetic  14.3 us (1%)
  between operations  13.8 us (1%)
  blocking collectives  12.7 us (1%)
    reduce_scatter x1, waiting for transfers between devices, body(): shared = lax.psum_scatter(key_terms, 'ctx', scatter_dimension=0, tiled=True)  329 us
    all_gather x1, waiting for transfers between devices, body(): lax.all_gather(value_rows, 'ctx', axis=0, tiled=True)  299 us
    all_gather x1, waiting for transfers between devices, body(): lax.all_gather(key_rows, 'ctx', axis=0, tiled=True)  297 us
    dynamic_slice x32, local copies, waits for them, and re-layouts, key_block(): key_pos = lax.dynamic_slice_in_dim(balance, row_start, block_len)  24.4 us
  transfers between devices with their start and end apart: 3, of which 3 were waited for; matrix products, arithmetic and copies ran while one was open for 1% of the time, Pallas kernels for 0%

commit v1 on v0

--- a/solution.py
+++ b/solution.py
@@ -26,7 +26,10 @@
     my_doc = lax.dynamic_slice_in_dim(docs_all, my_first, tok_rows)
     all_keys, all_values = (
         lax.all_gather(key_rows, "ctx", axis=0, tiled=True),
-        lax.all_gather(value_rows, "ctx", axis=0, tiled=True),
+        jnp.concatenate(
+            lax.all_to_all(jnp.stack(lax.axis_size("ctx") * [value_rows], axis=0), "ctx", 0, 0),
+            axis=0,
+        ),
     )
 
     def key_block(row_start):

time: 1130 us -> 850 us (0.75)
  waiting for transfers between devices: 927 us -> 617 us
  local copies, waits for them, and re-layouts: 51.9 us -> 75 us
  starting transfers between devices: 0.11 us -> 13.4 us
  matrix products: 110 us -> 97 us
    all_gather x1 -> x0, waiting for transfers between devices: 299 us -> none  [body(): lax.all_gather(value_rows, 'ctx', axis=0, tiled=True)]
    dynamic_slice x32, local copies, waits for them, and re-layouts: 2.37 us -> 24.3 us  [key_block(): key_doc = lax.dynamic_slice_in_dim(docs_all, row_start, block_len)]
    dot_general x16, matrix products: 19.1 us -> 4.52 us  [backward_tile(): jnp.einsum('qhd,kd->qhk', grad_part, value_blk, preferred_element_type=jn...]
    dot_general x16, matrix products: 21.6 us -> 7.14 us  [forward_step(): jnp.einsum('qhk,kd->qhd', raw_weights.astype(jnp.bfloat16), value_blk, pr...]
    dot_general x16, matrix products: 4.93 us -> 19.4 us  [query_step(): jnp.einsum('qhk,qhd->kd', grad_scores, queries, preferred_element_type=jn...]
    all_to_all x0 -> x1, starting transfers between devices: none -> 13.3 us  [body(): lax.all_to_all(jnp.stack(lax.axis_size('ctx') * [value_rows], axis=0), 'c...]
  transfers between devices with their start and end apart: 3 -> 3, of which waited for: 3 -> 2; matrix products, arithmetic and copies ran while one was open for 1% -> 1% of each run, Pallas kernels for 0% -> 0%
where the time goes in v1:
time: 850 us; the launch traced here: 846 us
  waiting for transfers between devices  617 us (73%)
  matrix products  97 us (11%)
  local copies, waits for them, and re-layouts  75 us (9%)
  other arithmetic  14.3 us (2%)
  between operations  14.1 us (2%)
  blocking collectives  13.8 us (2%)
  starting transfers between devices  13.4 us (2%)
    reduce_scatter x1, waiting for transfers between devices, body(): shared = lax.psum_scatter(key_terms, 'ctx', scatter_dimension=0, tiled=True)  328 us
    all_gather x1, waiting for transfers between devices, body(): lax.all_gather(key_rows, 'ctx', axis=0, tiled=True)  288 us
    dynamic_slice x32, local copies, waits for them, and re-layouts, key_block(): key_pos = lax.dynamic_slice_in_dim(balance, row_start, block_len)  24.4 us
    dynamic_slice x32, local copies, waits for them, and re-layouts, key_block(): key_doc = lax.dynamic_slice_in_dim(docs_all, row_start, block_len)  24.3 us
    dot_general x16, matrix products, backward_tile(): jnp.einsum('qhd,kd->qhk', query_part, key_blk, preferred_element_type=jnp...  21 us
    dot_general x16, matrix products, query_step(): jnp.einsum('qhk,kd->qhd', grad_scores, key_blk, preferred_element_type=jn...  20.5 us
    dot_general x16, matrix products, forward_step(): jnp.einsum('qhd,kd->qhk', queries, key_blk, preferred_element_type=jnp.fl...  19.6 us
    dot_general x16, matrix products, query_step(): jnp.einsum('qhk,qhd->kd', grad_scores, queries, preferred_element_type=jn...  19.4 us
  transfers between devices with their start and end apart: 3, of which 2 were waited for; matrix products, arithmetic and copies ran while one was open for 1% of the time, Pallas kernels for 0%

profile of v1, /device:TPU:2, one launch (start us, length us, event | category | flops | bytes accessed | tf_op | source)
XLA Modules:
  0.0 846.3 jit_solution(11324856530323034440)
XLA Ops:
  7.9 2.6 stack.2
  10.5 13.3 %all-to-all-start = ((bf16[64,128,128]{2,1,0:T(8,128)(2,1)}), bf16[64,128,128]{2,1,0:T(8,128)(2,1)S(1)}, u32[]{:S(2)}, u32[]{:S(2)}) async-start(bf16[64,128,128]{2,1,0:T(8,128)(2,1)} %stack.2), calls=%async_computation | async-start | bytes 4194304 | tf_op jit(solution)/shard_map/all_to_all | solution.py:30
  25.7 1.5 convert_reduce_fusion
  28.1 288.3 %all-gather.2.cloned.1.call-done = bf16[8192,128]{1,0:T(8,128)(2,1)} async-done(((bf16[128,128]{1,0:T(8,128)(2,1)}), bf16[8192,128]{1,0:T(8,128)(2,1)}) %all-gather.2.cloned.1.call-update) | async-done | bytes 2097168 | tf_op jit(solution)/shard_map/all_gather | solution.py:28
  316.4 59.0 %while.34 = (s32[]{:T(128)}, f32[128,4]{0,1:T(4,128)S(1)}, f32[128,4]{0,1:T(4,128)S(1)}, f32[128,4,128]{2,0,1:T(8,128)S(1)}, s32[8192]{0:T(1024)}, /*index=5*/s3...) while((s32[]{:T(128)}, f32[128,4]{0,1:T(4,128)S(1)}, ...), condition=%wide.region_5.6_spmd.clone, body=%wide.region_2.5_spmd.clone.sunk | while | flops 136972800 | bytes 4371679 | solution.py:71
  376.5 3.8 broadcast_in_dim.114.clone
  380.3 116.0 %while.35 = (s32[]{:T(128)}, f32[128,4,128]{2,0,1:T(8,128)S(1)}, f32[8192,256]{1,0:T(8,128)}, s32[8192]{0:T(1024)}, s32[128]{0:T(128)S(1)}, /*index=5*/s32[8192]...) while((s32[]{:T(128)}, f32[128,4,128]{2,0,1:T(8,128)S(1)}, ...), condition=%wide.region_8.9_spmd.clone, body=%wide.region_7.8_spmd.clone.sunk | while | flops 337903616 | bytes 9979125 | solution.py:115
  382.0 1.3 fusion.81
  389.3 1.3 fusion.81
  396.5 1.3 fusion.81
  411.1 1.3 fusion.81
  418.3 1.3 fusion.81
  425.6 1.3 fusion.81
  432.8 1.3 fusion.81
  440.1 1.3 fusion.81
  447.3 1.3 fusion.81
  454.6 1.3 fusion.81
  461.8 1.3 fusion.81
  469.1 1.3 fusion.81
  476.3 1.3 fusion.81
  483.6 1.3 fusion.81
  490.8 1.3 fusion.81
  497.2 327.7 %reduce-scatter.2.cloned.1.call-done = f32[128,256]{1,0:T(8,128)} async-done(((f32[8192,256]{1,0:T(8,128)}), f32[128,256]{1,0:T(8,128)}) %reduce-scatter.2.cloned.1.call-update) | async-done | bytes 131088 | tf_op jit(solution)/shard_map/reduce_scatter | solution.py:117
  824.9 13.8 %all-reduce.1 = bf16[128,256]{1,0:T(8,128)(2,1)S(1)} all-reduce(f32[128,256]{1,0:T(8,128)} %reduce-scatter.2.cloned.1.call-done), channel_id=1, replica_groups=mesh['seq'=2,'ctx'=64,'head'=2] {'head'}, use_global_device_ids=true, to_apply=%region_10.11 | all-reduce | flops 32768 | bytes 196608 | tf_op jit(solution)/shard_map/psum | solution.py:118
  (332 shorter events, 159.4 us)
Async XLA Ops:
  7.2 309.3 %all-gather.2.cloned.1.call-start = ((), (), s32[]{:S(2)}) async-start(), calls=%async_computation.2 | async-start | bytes 2129920 | tf_op jit(solution)/shard_map/all_gather | solution.py:28
  10.5 13.4 %copy-start.1 = (bf16[128,4,128]{2,1,0:T(4,128)(2,1)S(1)}, bf16[128,4,128]{2,1,0:T(4,128)(2,1)}, u32[]{:S(2)}) copy-start(bf16[128,4,128]{2,1,0:T(4,128)(2,1)} %param.10) | copy-start | bytes 393220
  10.5 14.3 %copy-start.2 = (s32[8]{0:T(128)S(1)}, s32[8]{0:T(128)}, u32[]{:S(2)}) copy-start(s32[8]{0:T(128)} %param.14) | copy-start | bytes 100
  10.5 17.5 %copy-start = (bf16[128,4,128]{2,1,0:T(4,128)(2,1)S(1)}, bf16[128,4,128]{2,1,0:T(4,128)(2,1)}, u32[]{:S(2)}) copy-start(bf16[128,4,128]{2,1,0:T(4,128)(2,1)} %param.13) | copy-start | bytes 393220
  10.5 305.9 %all-to-all-start = ((bf16[64,128,128]{2,1,0:T(8,128)(2,1)}), bf16[64,128,128]{2,1,0:T(8,128)(2,1)S(1)}, u32[]{:S(2)}, u32[]{:S(2)}) async-start(bf16[64,128,128]{2,1,0:T(8,128)(2,1)} %stack.2), calls=%async_computation | async-start | bytes 4194304 | tf_op jit(solution)/shard_map/all_to_all | solution.py:30
  23.9 801.1 %reduce-scatter.2.cloned.1.call-start = ((), (), s32[]{:S(2)}) async-start(), calls=%async_computation.3 | async-start | bytes 8519680 | tf_op jit(solution)/shard_map/reduce_scatter | solution.py:117
Sparse Core Ops, SparseCore 0:
  9.8 306.5 all-gather.1
  496.5 328.4 reduce-scatter.1
